TPU v7x, 512 devices: a whole 4x4x16 slice. The times are simulated.
512 devices in a mesh: row: 16 (over y, x_lo, core), col: 32 (over z, x_hi).
Axes of the slice: x: 4 (x_hi: 2, x_lo: 2; x = x_hi * 2 + x_lo), y: 4, z: 16, core: 2. Of those that a mesh axis runs over, the one named last changes fastest.
Arguments:
- traces: float32 [1024, 4096], P(('row', 'col')), may hold values from -6 to 6
- offsets: int32 [1024, 8], P(('row', 'col')), may hold values from 0 to 3072, as said below
- band_lo: int32 [1024], P(('row', 'col')), may hold values from 0 to 63
- band_hi: int32 [1024], P(('row', 'col')), may hold values from 192 to 256
- live: int32 [1024], P(('row', 'col')), may hold values 0 or 1
Outputs:
- correlations: bfloat16 [1024, 32, 16, 2, 512], P('row', 'col')
Inputs may be any that keep to these rules, and one draw needn't show every extreme that they name: `offsets`: every offset is a multiple of 256.
All inputs are finite; a program needn't handle non-finite values. No bound on the sum of `live` on one device may be relied on, other than what follows from the above.
Results may differ from a plain program's by a relative error of at most 0.0052.
Values may be sent and summed in bfloat16 or wider, within the bound.
A program may use at most 64 MiB of HBM per device.

v0:
```python
import math
import jax
import jax.numpy as jnp
from jax import lax
from jax.sharding import PartitionSpec as P

SEG = 8
SAMPLES = 1024
BINS = 256
LAGS = 512
TRACE = 4096


def sent_to_all(x, axis):
    devices = lax.axis_size(axis)
    return lax.all_to_all(jnp.broadcast_to(x[None], (devices, *x.shape)), axis, 0, 0, tiled=True)


def laid_out(pieces, dim):
    dims = list(pieces.shape[1:])
    dims[dim] *= pieces.shape[0]
    return jnp.moveaxis(pieces, 0, dim).reshape(dims)


def gather_directly(x, axis, dim):
    pieces = sent_to_all(x, axis)
    return laid_out(pieces, dim)


def transform_table():
    times = jnp.arange(SAMPLES, dtype=jnp.int32)
    freqs = jnp.arange(BINS, dtype=jnp.int32) + 1
    phase = jnp.mod(times[:, None] * freqs[None, :], SAMPLES).astype(jnp.float32) * (
        2.0 * math.pi / SAMPLES
    )
    taper = 0.5 - 0.5 * jnp.cos(times.astype(jnp.float32) * (2.0 * math.pi / SAMPLES))
    return jnp.concatenate([jnp.cos(phase), -jnp.sin(phase)], axis=1) * taper[:, None]


def lag_table():
    freqs = jnp.arange(BINS, dtype=jnp.int32) + 1
    shifts = jnp.arange(LAGS, dtype=jnp.int32) - LAGS // 2
    phase = jnp.mod(freqs[:, None] * shifts[None, :], SAMPLES).astype(jnp.float32) * (
        2.0 * math.pi / SAMPLES
    )
    return jnp.concatenate([jnp.cos(phase), -jnp.sin(phase)], axis=0) * (
        1.0 / math.sqrt(SEG * BINS)
    )


def cut_segments(traces, offsets):
    count = traces.shape[0]
    quarter = SAMPLES // 4
    block_count = TRACE // quarter
    blocks = traces.reshape(count, 1, block_count, quarter)
    first_block = offsets // quarter
    segment = jnp.zeros((count, SEG, 4, quarter), jnp.float32)
    for place in range(block_count - 3):
        picked = (first_block == place)[:, :, None, None]
        segment = jnp.where(picked, blocks[:, :, place : place + 4, :], segment)
    return segment.reshape(count * SEG, SAMPLES)


def whiten(traces, offsets, band_lo, band_hi, live):
    count = traces.shape[0]
    flat = cut_segments(traces, offsets)
    spec = jnp.dot(flat, transform_table(), precision=lax.Precision.HIGHEST)
    spec_re = spec[:, :BINS]
    spec_im = spec[:, BINS:]
    amp = jnp.sqrt(spec_re * spec_re + spec_im * spec_im)
    padded = jnp.pad(amp, ((0, 0), (2, 2)))
    smooth = (
        padded[:, 0:BINS]
        + padded[:, 1 : BINS + 1]
        + padded[:, 2 : BINS + 2]
        + padded[:, 3 : BINS + 3]
        + padded[:, 4 : BINS + 4]
    ) / 5.0
    level = jnp.mean(amp, axis=1, keepdims=True)
    factor = 1.0 / (smooth + 0.1 * level + 1e-06)
    bins = jnp.arange(BINS, dtype=jnp.int32)
    inside = (
        (bins[None, :] >= band_lo[:, None])
        & (bins[None, :] < band_hi[:, None])
        & (live[:, None] == 1)
    )
    keep = inside.astype(jnp.float32)
    factor = factor.reshape(count, SEG, BINS) * keep[:, None, :]
    spec = spec.reshape(count, SEG, 2 * BINS)
    white = spec * jnp.concatenate([factor, factor], axis=2)
    return white.astype(jnp.bfloat16)


def correlate(first, second, table):
    first_re, first_im = (first[..., :BINS], first[..., BINS:])
    second_re, second_im = (second[..., :BINS], second[..., BINS:])
    count_i, count_j = (first.shape[0], second.shape[0])
    cross_re = jnp.zeros((count_i, count_j, BINS), jnp.float32)
    cross_im = jnp.zeros((count_i, count_j, BINS), jnp.float32)
    for seg_index in range(SEG):
        left_re = first_re[:, None, seg_index, :].astype(jnp.float32)
        left_im = first_im[:, None, seg_index, :].astype(jnp.float32)
        right_re = second_re[None, :, seg_index, :].astype(jnp.float32)
        right_im = second_im[None, :, seg_index, :].astype(jnp.float32)
        cross_re = cross_re + (left_re * right_re + left_im * right_im)
        cross_im = cross_im + (left_im * right_re - left_re * right_im)
    cross = jnp.concatenate([cross_re, cross_im], axis=2)
    corr = jnp.dot(
        cross.reshape(count_i * count_j, 2 * BINS), table, precision=lax.Precision.HIGHEST
    )
    return corr.astype(jnp.bfloat16).reshape(count_i, count_j, LAGS)


def body(traces, offsets, band_lo, band_hi, live):
    white = whiten(traces, offsets, band_lo, band_hi, live)
    table = lag_table()
    first_panel = gather_directly(white, "col", 0)
    stacked = correlate(first_panel, lax.all_gather(white, "row", axis=0, tiled=True), table)
    channel_count = white.shape[0]
    return stacked.reshape(stacked.shape[0], 1, lax.axis_size("row"), channel_count, LAGS)


def solution(mesh):
    in_specs = (
        P(("row", "col"), None),
        P(("row", "col"), None),
        P(("row", "col")),
        P(("row", "col")),
        P(("row", "col")),
    )
    out_specs = P("row", "col", None, None, None)
    return jax.shard_map(body, mesh=mesh, in_specs=in_specs, out_specs=out_specs, check_vma=False)
```

profile of v0, /device:TPU:24, one launch (start us, length us, event | category | flops | bytes accessed | tf_op | source)
XLA Modules:
  0.0 75.8 jit_solution(12472655420938415955)
XLA Ops:
  0.0 0.7 broadcast_compare_fusion.13
  0.7 0.7 broadcast_compare_fusion.9
  1.4 0.1 broadcast_in_dim.248
  1.5 0.1 broadcast_in_dim.253
  1.6 0.1 broadcast_in_dim.303
  1.7 0.1 broadcast_in_dim.298
  1.8 0.1 broadcast_in_dim.293
  1.8 0.1 broadcast_in_dim.288
  1.9 0.1 broadcast_in_dim.283
  2.0 0.1 broadcast_in_dim.278
  2.1 0.1 broadcast_in_dim.273
  2.2 0.1 broadcast_in_dim.268
  2.3 0.1 broadcast_in_dim.263
  2.4 0.1 broadcast_in_dim.258
  2.4 0.1 broadcast_in_dim.308
  2.5 0.8 %copy.74 = f32[1,2,16,256]{3,2,1,0:T(8,128)S(1)} copy(f32[1,2,16,256]{3,1,2,0:T(2,128)} %bitcast.134) | data formatting | bytes 65536
  3.3 4.1 %fusion.23 = (f32[1024,256]{1,0:T(8,128)S(1)}, f32[1024,256]{1,0:T(8,128)S(1)}) fusion(s32[256]{0:T(256)S(1)} %iota_add_fusion.1), kind=kLoop, calls=%fused_computation.35 | loop fusion | flops 3932160 | bytes 2098176 | tf_op jit(solution)/shard_map/cos | solution.py:37
  7.4 0.0 copy-start
  7.4 0.0 copy-start.1
  7.6 1.3 %fusion.7 = f32[16,512]{1,0:T(8,128)S(1)} fusion(f32[1024,256]{1,0:T(8,128)S(1)} %get-tuple-element.69, f32[1024,256]{1,0:T(8,128)S(1)} %get-tuple-element.68, f32[1024]{0:T(1024)S(1)} %multiply_subtract_fusion, f32[16,1024]{1,0:T(8,128)S(1)} %bitcast.133, f32[16,1024]{1,0:T(8,128)S(1)} %bitcast.132, f32[16,1024]{1,0:T(8,128)S(1)} %bitcast.131, ...), kind=kOutput, calls=%fused_computation.6 | convolution fusion | flops 101924864 | bytes 2986192 | tf_op jit(solution)/shard_map/dot_general | solution.py:67
  9.0 0.1 fusion.67
  9.1 0.0 copy-done
  9.1 0.0 copy-done.1
  9.1 0.1 and_convert_fusion
  9.2 0.1 bitcast_multiply_fusion
  9.3 0.9 %broadcast_in_dim.314 = bf16[32,2,8,512]{3,2,1,0:T(8,128)(2,1)} broadcast(bf16[2,8,512]{2,1,0:T(8,128)(2,1)S(1)} %fusion.38), dimensions={1,2,3} | broadcast | bytes 540672 | tf_op jit(solution)/shard_map/broadcast_in_dim | solution.py:16
  10.2 17.9 %all-to-all-start = ((bf16[32,2,8,512]{3,2,1,0:T(8,128)(2,1)}), bf16[32,2,8,512]{3,2,1,0:T(8,128)(2,1)S(1)}, u32[]{:S(2)}, u32[]{:S(2)}) async-start(bf16[32,2,8,512]{3,2,1,0:T(8,128)(2,1)} %broadcast_in_dim.314), calls=%async_computation | async-start | bytes 1048576 | tf_op jit(solution)/shard_map/all_to_all | solution.py:16
  28.1 17.6 %all_gather.3 = bf16[32,8,512]{2,1,0:T(8,128)(2,1)S(1)} all-gather(bf16[2,8,512]{2,1,0:T(8,128)(2,1)S(1)} %fusion.38), channel_id=1, replica_groups=mesh['row'=16,'col'=32] {'row'}, dimensions={0}, use_global_device_ids=true | all-gather | bytes 278528 | tf_op jit(solution)/shard_map/all_gather | solution.py:118
  45.7 0.5 slice_convert_fusion.31
  46.3 2.1 %fusion.24 = (f32[256,512]{1,0:T(8,128)S(1)}, f32[256,512]{1,0:T(8,128)S(1)}) fusion(s32[512]{0:T(512)S(1)} %iota_add_fusion, s32[256]{0:T(256)S(1)} %iota_add_fusion.1), kind=kLoop, calls=%fused_computation.36 | loop fusion | flops 1966080 | bytes 1051648 | tf_op jit(solution)/shard_map/cos | solution.py:46
  48.4 12.7 %all-to-all-done = bf16[32,2,8,512]{3,2,1,0:T(8,128)(2,1)S(1)} async-done(((bf16[32,2,8,512]{3,2,1,0:T(8,128)(2,1)}), bf16[32,2,8,512]{3,2,1,0:T(8,128)(2,1)S(1)}, u32[]{:S(2)}, u32[]{:S(2)}) %all-to-all-start) | async-done | bytes 524320 | tf_op jit(solution)/shard_map/all_to_all | solution.py:16
  61.1 1.0 %slice_convert_fusion.15 = (f32[64,1,256]{2,1,0:T(1,128)S(1)}, f32[64,1,256]{2,1,0:T(1,128)S(1)}, f32[64,1,256]{2,1,0:T(1,128)S(1)}, f32[64,1,256]{2,1,0:T(1,128...) fusion(bf16[64,8,512]{2,1,0:T(8,128)(2,1)S(1)} %bitcast.117), kind=kLoop, calls=%fused_computation.52 | loop fusion | flops 262144 | bytes 1572864 | tf_op jit(solution)/shard_map/mul | solution.py:105
  62.2 2.2 %add_add_fusion = f32[64,32,256]{2,1,0:T(8,128)S(1)} fusion(f32[32,256]{1,0:T(8,128)S(1)} %get-tuple-element.70, f32[64,256]{1,0:T(8,128)S(1)} %get-tuple-element.86, f32[32,256]{1,0:T(8,128)S(1)} %get-tuple-element.71, f32[64,256]{1,0:T(8,128)S(1)} %get-tuple-element.87, f32[32,256]{1,0:T(8,128)S(1)} %get-tuple-element.72, ...), kind=kLoop, calls=%fused_computation.9 | loop fusion | flops 16252928 | bytes 3670016 | tf_op jit(solution)/shard_map/add | solution.py:106
  64.4 2.2 %add_add_fusion.1 = f32[64,32,256]{2,1,0:T(8,128)S(1)} fusion(f32[32,256]{1,0:T(8,128)S(1)} %get-tuple-element.70, f32[64,256]{1,0:T(8,128)S(1)} %get-tuple-element.86, f32[32,256]{1,0:T(8,128)S(1)} %get-tuple-element.71, f32[64,256]{1,0:T(8,128)S(1)} %get-tuple-element.87, f32[32,256]{1,0:T(8,128)S(1)} %get-tuple-element.72, ...), kind=kLoop, calls=%fused_computation.10 | loop fusion | flops 16252928 | bytes 3670016 | tf_op jit(solution)/shard_map/add | solution.py:105
  66.7 7.0 %fusion.4 = bf16[2048,512]{1,0:T(8,128)(2,1)S(1)} fusion(f32[2048,256]{1,0:T(8,128)S(1)} %bitcast.118, f32[2048,256]{1,0:T(8,128)S(1)} %bitcast.119, f32[256,512]{1,0:T(8,128)S(1)} %get-tuple-element.55, f32[256,512]{1,0:T(8,128)S(1)} %get-tuple-element.54), kind=kOutput, calls=%fused_computation.4 | convolution fusion | flops 6445072384 | bytes 7340032 | tf_op jit(solution)/shard_map/dot_general | solution.py:108
  73.6 2.2 %reshape_reshape.3 = bf16[64,1,16,2,512]{4,3,2,0,1:T(2,128)(2,1)} reshape(bf16[2048,512]{1,0:T(8,128)(2,1)S(1)} %fusion.4) | data formatting | bytes 4194304 | tf_op jit(solution)/shard_map/reshape;reshape | solution.py:120
  (36 shorter events, 0.3 us)
Async XLA Ops:
  7.4 1.7 %copy-start = (s32[2]{0:T(128)S(1)}, s32[2]{0:T(128)}, u32[]{:S(2)}) copy-start(s32[2]{0:T(128)} %param.8) | copy-start | bytes 28
  7.4 1.7 %copy-start.1 = (s32[2]{0:T(128)S(1)}, s32[2]{0:T(128)}, u32[]{:S(2)}) copy-start(s32[2]{0:T(128)} %param.7) | copy-start | bytes 28
  10.2 51.0 %all-to-all-start = ((bf16[32,2,8,512]{3,2,1,0:T(8,128)(2,1)}), bf16[32,2,8,512]{3,2,1,0:T(8,128)(2,1)S(1)}, u32[]{:S(2)}, u32[]{:S(2)}) async-start(bf16[32,2,8,512]{3,2,1,0:T(8,128)(2,1)} %broadcast_in_dim.314), calls=%async_computation | async-start | bytes 1048576 | tf_op jit(solution)/shard_map/all_to_all | solution.py:16
where the time goes:
time: 76.1 us; the launch traced here: 75.8 us
  starting transfers between devices  17.9 us (24%)
  blocking collectives  17.6 us (23%)
  other arithmetic  13.8 us (18%)
  waiting for transfers between devices  12.7 us (17%)
  matrix products  8.27 us (11%)
  local copies, waits for them, and re-layouts  5.18 us (7%)
    all_to_all x1, starting transfers between devices, sent_to_all(): lax.all_to_all(jnp.broadcast_to(x[None], (devices, *x.shape)), axis, 0, 0...  17.9 us
    all_gather x1, blocking collectives, body(): lax.all_gather(white, 'row', axis=0, tiled=True)  17.6 us
    all_to_all x1, waiting for transfers between devices, sent_to_all(): lax.all_to_all(jnp.broadcast_to(x[None], (devices, *x.shape)), axis, 0, 0...  12.7 us
    dot_general x1, matrix products, correlate(): jnp.dot(cross.reshape(count_i * count_j, 2 * BINS), table, precision=lax....  6.96 us
    cos x1, other arithmetic, transform_table(): jnp.cos(phase)  4.13 us
    another operation x1, local copies, waits for them, and re-layouts, body(): stacked.reshape(stacked.shape[0], 1, lax.axis_size('row'), channel_count,...  2.21 us
    add x1, other arithmetic, correlate(): cross_im = cross_im + (left_im * right_re - left_re * right_im)  2.21 us
    add x1, other arithmetic, correlate(): cross_re = cross_re + (left_re * right_re + left_im * right_im)  2.21 us
  transfers between devices with their start and end apart: 1, of which 1 were waited for; matrix products, arithmetic and copies ran while one was open for 4% of the time, Pallas kernels for 0%

commit v1 on v0

--- a/solution.py
+++ b/solution.py
@@ -9,6 +9,11 @@
 BINS = 256
 LAGS = 512
 TRACE = 4096
+
+
+def exchange_gather(x, mesh_axis, along):
+    sent = jnp.stack([x] * lax.axis_size(mesh_axis))
+    return jnp.concatenate(lax.all_to_all(sent, mesh_axis, 0, 0), axis=along)
 
 
 def sent_to_all(x, axis):
@@ -115,7 +120,7 @@
     white = whiten(traces, offsets, band_lo, band_hi, live)
     table = lag_table()
     first_panel = gather_directly(white, "col", 0)
-    stacked = correlate(first_panel, lax.all_gather(white, "row", axis=0, tiled=True), table)
+    stacked = correlate(first_panel, exchange_gather(white, "row", 0), table)
     channel_count = white.shape[0]
     return stacked.reshape(stacked.shape[0], 1, lax.axis_size("row"), channel_count, LAGS)
 

time: 76.1 us -> 90.1 us (1.18)
  the two profiles are of different devices: /device:TPU:24 before, /device:TPU:4 now
where the time goes in v1:
time: 90.1 us; the launch traced here: 89.7 us
  waiting for transfers between devices  37.7 us (42%)
  starting transfers between devices  23.4 us (26%)
  other arithmetic  13.8 us (15%)
  matrix products  8.27 us (9%)
  local copies, waits for them, and re-layouts  6.13 us (7%)
    all_to_all x1, waiting for transfers between devices, sent_to_all(): lax.all_to_all(jnp.broadcast_to(x[None], (devices, *x.shape)), axis, 0, 0...  31.8 us
    all_to_all x1, starting transfers between devices, sent_to_all(): lax.all_to_all(jnp.broadcast_to(x[None], (devices, *x.shape)), axis, 0, 0...  18.2 us
    dot_general x1, matrix products, correlate(): jnp.dot(cross.reshape(count_i * count_j, 2 * BINS), table, precision=lax....  6.96 us
    all_to_all x1, waiting for transfers between devices, exchange_gather(): return jnp.concatenate(lax.all_to_all(sent, mesh_axis, 0, 0), axis=along)  5.87 us
    all_to_all x1, starting transfers between devices, exchange_gather(): return jnp.concatenate(lax.all_to_all(sent, mesh_axis, 0, 0), axis=along)  5.21 us
    cos x1, other arithmetic, transform_table(): jnp.cos(phase)  4.13 us
    another operation x1, local copies, waits for them, and re-layouts, body(): stacked.reshape(stacked.shape[0], 1, lax.axis_size('row'), channel_count,...  2.21 us
    add x1, other arithmetic, correlate(): cross_im = cross_im + (left_im * right_re - left_re * right_im)  2.21 us
  transfers between devices with their start and end apart: 2, of which 2 were waited for; matrix products, arithmetic and copies ran while one was open for 3% of the time, Pallas kernels for 0%

profile of v1, /device:TPU:4, one launch (start us, length us, event | category | flops | bytes accessed | tf_op | source)
XLA Modules:
  0.0 89.7 jit_solution(15936133761434163184)
XLA Ops:
  0.0 0.7 broadcast_compare_fusion.13
  0.7 0.7 broadcast_compare_fusion.9
  1.4 0.1 broadcast_in_dim.248
  1.5 0.1 broadcast_in_dim.253
  1.6 0.1 broadcast_in_dim.303
  1.7 0.1 broadcast_in_dim.298
  1.8 0.1 broadcast_in_dim.293
  1.8 0.1 broadcast_in_dim.288
  1.9 0.1 broadcast_in_dim.283
  2.0 0.1 broadcast_in_dim.278
  2.1 0.1 broadcast_in_dim.273
  2.2 0.1 broadcast_in_dim.268
  2.3 0.1 broadcast_in_dim.263
  2.4 0.1 broadcast_in_dim.258
  2.4 0.1 broadcast_in_dim.308
  2.5 0.8 copy.79
  3.3 4.1 %fusion.23 = (f32[1024,256]{1,0:T(8,128)S(1)}, f32[1024,256]{1,0:T(8,128)S(1)}) fusion(s32[256]{0:T(256)S(1)} %iota_add_fusion.1), kind=kLoop, calls=%fused_computation.35 | loop fusion | flops 3932160 | bytes 2098176 | tf_op jit(solution)/shard_map/cos | solution.py:42
  7.4 0.0 copy-start
  7.4 0.0 copy-start.1
  7.6 1.3 %fusion.7 = f32[16,512]{1,0:T(8,128)S(1)} fusion(f32[1024,256]{1,0:T(8,128)S(1)} %get-tuple-element.69, f32[1024,256]{1,0:T(8,128)S(1)} %get-tuple-element.68, f32[1024]{0:T(1024)S(1)} %multiply_subtract_fusion, f32[16,1024]{1,0:T(8,128)S(1)} %bitcast.135, f32[16,1024]{1,0:T(8,128)S(1)} %bitcast.134, f32[16,1024]{1,0:T(8,128)S(1)} %bitcast.133, ...), kind=kOutput, calls=%fused_computation.6 | convolution fusion | flops 101924864 | bytes 2986192 | tf_op jit(solution)/shard_map/dot_general | solution.py:72
  9.0 0.1 fusion.67
  9.1 0.0 copy-done
  9.1 0.0 copy-done.1
  9.1 0.1 and_convert_fusion
  9.2 0.1 bitcast_multiply_fusion
  9.3 0.9 %stack.2 = bf16[16,2,8,512]{3,1,2,0:T(2,128)(2,1)} broadcast(bf16[2,8,512]{2,0,1:T(2,128)(2,1)S(1)} %copy.10), dimensions={1,2,3} | broadcast | bytes 278528 | tf_op jit(solution)/shard_map/stack | solution.py:15
  10.2 5.2 %all-to-all-start.1 = ((bf16[16,2,8,512]{3,1,2,0:T(2,128)(2,1)}), bf16[16,2,8,512]{3,1,2,0:T(2,128)(2,1)S(1)}, u32[]{:S(2)}, u32[]{:S(2)}) async-start(bf16[16,2,8,512]{3,1,2,0:T(2,128)(2,1)} %stack.2), calls=%async_computation.1 | async-start | bytes 524288 | tf_op jit(solution)/shard_map/all_to_all | solution.py:16
  15.5 2.1 %fusion.24 = (f32[256,512]{1,0:T(8,128)S(1)}, f32[256,512]{1,0:T(8,128)S(1)}) fusion(s32[512]{0:T(512)S(1)} %iota_add_fusion, s32[256]{0:T(256)S(1)} %iota_add_fusion.1), kind=kLoop, calls=%fused_computation.36 | loop fusion | flops 1966080 | bytes 1051648 | tf_op jit(solution)/shard_map/cos | solution.py:51
  17.6 5.9 %all-to-all-done.1 = bf16[16,2,8,512]{3,1,2,0:T(2,128)(2,1)S(1)} async-done(((bf16[16,2,8,512]{3,1,2,0:T(2,128)(2,1)}), bf16[16,2,8,512]{3,1,2,0:T(2,128)(2,1)S(1)}, u32[]{:S(2)}, u32[]{:S(2)}) %all-to-all-start.1) | async-done | bytes 262176 | tf_op jit(solution)/shard_map/all_to_all | solution.py:16
  23.5 0.9 broadcast_in_dim.314
  24.3 18.2 %all-to-all-start = ((bf16[32,2,8,512]{3,2,1,0:T(8,128)(2,1)}), bf16[32,2,8,512]{3,2,1,0:T(8,128)(2,1)S(1)}, u32[]{:S(2)}, u32[]{:S(2)}) async-start(bf16[32,2,8,512]{3,2,1,0:T(8,128)(2,1)} %broadcast_in_dim.314), calls=%async_computation | async-start | bytes 1048576 | tf_op jit(solution)/shard_map/all_to_all | solution.py:21
  42.6 0.5 slice_convert_fusion.31
  43.2 31.8 %all-to-all-done = bf16[32,2,8,512]{3,2,1,0:T(8,128)(2,1)S(1)} async-done(((bf16[32,2,8,512]{3,2,1,0:T(8,128)(2,1)}), bf16[32,2,8,512]{3,2,1,0:T(8,128)(2,1)S(1)}, u32[]{:S(2)}, u32[]{:S(2)}) %all-to-all-start) | async-done | bytes 524320 | tf_op jit(solution)/shard_map/all_to_all | solution.py:21
  75.0 1.0 %slice_convert_fusion.15 = (f32[64,1,256]{2,1,0:T(1,128)S(1)}, f32[64,1,256]{2,1,0:T(1,128)S(1)}, f32[64,1,256]{2,1,0:T(1,128)S(1)}, f32[64,1,256]{2,1,0:T(1,128...) fusion(bf16[64,8,512]{2,1,0:T(8,128)(2,1)S(1)} %bitcast.118), kind=kLoop, calls=%fused_computation.52 | loop fusion | flops 262144 | bytes 1572864 | tf_op jit(solution)/shard_map/mul | solution.py:110
  76.1 2.2 %add_add_fusion = f32[64,32,256]{2,1,0:T(8,128)S(1)} fusion(f32[32,256]{1,0:T(8,128)S(1)} %get-tuple-element.70, f32[64,256]{1,0:T(8,128)S(1)} %get-tuple-element.86, f32[32,256]{1,0:T(8,128)S(1)} %get-tuple-element.71, f32[64,256]{1,0:T(8,128)S(1)} %get-tuple-element.87, f32[32,256]{1,0:T(8,128)S(1)} %get-tuple-element.72, ...), kind=kLoop, calls=%fused_computation.9 | loop fusion | flops 16252928 | bytes 3670016 | tf_op jit(solution)/shard_map/add | solution.py:111
  78.3 2.2 %add_add_fusion.1 = f32[64,32,256]{2,1,0:T(8,128)S(1)} fusion(f32[32,256]{1,0:T(8,128)S(1)} %get-tuple-element.70, f32[64,256]{1,0:T(8,128)S(1)} %get-tuple-element.86, f32[32,256]{1,0:T(8,128)S(1)} %get-tuple-element.71, f32[64,256]{1,0:T(8,128)S(1)} %get-tuple-element.87, f32[32,256]{1,0:T(8,128)S(1)} %get-tuple-element.72, ...), kind=kLoop, calls=%fused_computation.10 | loop fusion | flops 16252928 | bytes 3670016 | tf_op jit(solution)/shard_map/add | solution.py:110
  80.5 7.0 %fusion.4 = bf16[2048,512]{1,0:T(8,128)(2,1)S(1)} fusion(f32[2048,256]{1,0:T(8,128)S(1)} %bitcast.120, f32[2048,256]{1,0:T(8,128)S(1)} %bitcast.121, f32[256,512]{1,0:T(8,128)S(1)} %get-tuple-element.55, f32[256,512]{1,0:T(8,128)S(1)} %get-tuple-element.54), kind=kOutput, calls=%fused_computation.4 | convolution fusion | flops 6445072384 | bytes 7340032 | tf_op jit(solution)/shard_map/dot_general | solution.py:113
  87.5 2.2 %reshape_reshape.3 = bf16[64,1,16,2,512]{4,3,2,0,1:T(2,128)(2,1)} reshape(bf16[2048,512]{1,0:T(8,128)(2,1)S(1)} %fusion.4) | data formatting | bytes 4194304 | tf_op jit(solution)/shard_map/reshape;reshape | solution.py:125
  (38 shorter events, 0.4 us)
Async XLA Ops:
  7.4 1.7 %copy-start = (s32[2]{0:T(128)S(1)}, s32[2]{0:T(128)}, u32[]{:S(2)}) copy-start(s32[2]{0:T(128)} %param.8) | copy-start | bytes 28
  7.4 1.7 %copy-start.1 = (s32[2]{0:T(128)S(1)}, s32[2]{0:T(128)}, u32[]{:S(2)}) copy-start(s32[2]{0:T(128)} %param.7) | copy-start | bytes 28
  10.2 13.2 %all-to-all-start.1 = ((bf16[16,2,8,512]{3,1,2,0:T(2,128)(2,1)}), bf16[16,2,8,512]{3,1,2,0:T(2,128)(2,1)S(1)}, u32[]{:S(2)}, u32[]{:S(2)}) async-start(bf16[16,2,8,512]{3,1,2,0:T(2,128)(2,1)} %stack.2), calls=%async_computation.1 | async-start | bytes 524288 | tf_op jit(solution)/shard_map/all_to_all | solution.py:16
  24.3 50.7 %all-to-all-start = ((bf16[32,2,8,512]{3,2,1,0:T(8,128)(2,1)}), bf16[32,2,8,512]{3,2,1,0:T(8,128)(2,1)S(1)}, u32[]{:S(2)}, u32[]{:S(2)}) async-start(bf16[32,2,8,512]{3,2,1,0:T(8,128)(2,1)} %broadcast_in_dim.314), calls=%async_computation | async-start | bytes 1048576 | tf_op jit(solution)/shard_map/all_to_all | solution.py:21
